TPU v7x, 256 devices: a whole 4x4x8 slice. The times are simulated.
256 devices in a mesh: dp: 8 (over x, core), seq: 32 (over z, y).
Axes of the slice: x: 4, y: 4, z: 8, core: 2. Of those that a mesh axis runs over, the one named last changes fastest.
Arguments:
- queries: bfloat16 [8, 8192, 2048], P('dp', 'seq'), may hold values from -40 to 40
- keys: bfloat16 [8, 8192, 2048], P('dp', 'seq'), may hold values from -40 to 40
- values: bfloat16 [8, 8192, 2048], P('dp', 'seq'), may hold values from -6 to 6
- key_gain: float32 [2048], replicated, may hold values from 0.25 to 1.75
- random_blocks: int32 [16, 128, 3], P(None, 'seq'), may hold values from 2 to 127, as said below
- out_grad: bfloat16 [8, 8192, 2048], P('dp', 'seq'), may hold values from -6 to 6
Outputs:
- attended: bfloat16 [8, 8192, 2048], P('dp', 'seq')
- query_grad: bfloat16 [8, 8192, 2048], P('dp', 'seq')
- key_grad: bfloat16 [8, 8192, 2048], P('dp', 'seq')
- value_grad: bfloat16 [8, 8192, 2048], P('dp', 'seq')
- gain_grad: float32 [2048], replicated
Inputs may be any that keep to these rules, and one draw needn't show every extreme that they name: `random_blocks`: for the 4 query blocks of one device, all heads and entries together, at most 9 entries name blocks held by any one device (blocks d * 4 to d * 4 + 3), and exactly 9 name the blocks of some device.
All inputs are finite; a program needn't handle non-finite values.
Results may differ from a plain program's by a relative error of at most 0.03.
The roundings to bfloat16 on the way count: a program that leaves them out, or rounds other values in their place, can miss the bound.
Values may be sent and summed in bfloat16 or wider, within the bound.
No kernel may reach another device: no remote copies, remote signals or barrier semaphores. Data moves between devices by JAX's collectives and lax.ppermute only.
A program may use at most 128 MiB of HBM per device.

v0:
```python
import math
import jax
import jax.numpy as jnp
from jax import lax
from jax.sharding import PartitionSpec as P

HEADS = 16
HD = 128
BLOCK = 64
NG = 2
NR = 3
NK = 8
NEGATIVE = -1e30


def broadcast(block, axis, owner):
    block = jnp.where(lax.axis_index(axis) == owner, block, jnp.zeros_like(block))
    return lax.psum(block, axis)


def padded_2(cells, sides, width):
    for axis, dim in sides:
        count = lax.axis_size(axis)
        ends = count - 1
        head = lax.slice_in_dim(cells, 0, width, axis=dim)
        tail = lax.slice_in_dim(cells, cells.shape[dim] - width, cells.shape[dim], axis=dim)
        cells = jnp.concatenate(
            [
                lax.ppermute(tail, axis, [(i, (i + 1) % count) for i in range(ends)]),
                cells,
                lax.ppermute(head, axis, [((i + 1) % count, i) for i in range(ends)]),
            ],
            axis=dim,
        )
    return cells


def passed_along(array, axis, by):
    length = lax.axis_size(axis)
    pairs = [(i, i + by) for i in range(length) if 0 <= i + by < length]
    return lax.ppermute(array, axis, pairs)


def to_heads(rows_in):
    return rows_in.reshape(rows_in.shape[0] // BLOCK, BLOCK, HEADS, HD).transpose(2, 0, 1, 3)


def from_heads(blocks_in):
    return blocks_in.transpose(1, 2, 0, 3).reshape(1, blocks_in.shape[1] * BLOCK, HEADS * HD)


def build_list(edge_part, window_part, random_in):
    head_count = random_in.shape[0]
    block_count = random_in.shape[1]
    global_list = jnp.broadcast_to(
        edge_part[:, None], (head_count, block_count) + edge_part.shape[1:]
    )
    window_list = jnp.stack(
        [window_part[:, offset : offset + block_count] for offset in range(3)], axis=2
    )
    joined = jnp.concatenate([global_list, window_list, random_in], axis=2)
    return joined.reshape(head_count, block_count, NK * BLOCK, HD)


def spread_terms(coef, rows_in):
    head_count = rows_in.shape[0]
    block_count = rows_in.shape[1]
    coef_blocks = coef.reshape(head_count, block_count, BLOCK, NK, BLOCK)
    global_term = jnp.einsum(
        "hpbgc,hpbd->hgcd", coef_blocks[:, :, :, :NG], rows_in, preferred_element_type=jnp.float32
    )
    padded = jnp.zeros((head_count, block_count + 2, BLOCK, HD), jnp.float32)
    for offset in range(3):
        term = jnp.einsum(
            "hpbc,hpbd->hpcd",
            coef_blocks[:, :, :, NG + offset],
            rows_in,
            preferred_element_type=jnp.float32,
        )
        padded = padded + jnp.pad(term, ((0, 0), (offset, 2 - offset), (0, 0), (0, 0)))
    random_term = jnp.einsum(
        "hpbrc,hpbd->hprcd",
        coef_blocks[:, :, :, NG + 3 :],
        rows_in,
        preferred_element_type=jnp.float32,
    )
    return (global_term, padded, random_term)


def sparse_group(
    query_blk,
    edge_key,
    edge_value,
    window_key,
    window_value,
    random_key,
    random_value,
    grad_blk,
    valid_keys,
    keep_rows,
):
    score_scale = HD ** (-0.5)
    key_list = build_list(edge_key, window_key, random_key)
    value_list = build_list(edge_value, window_value, random_value)
    key_mask = jnp.repeat(valid_keys, BLOCK, axis=1)[None, :, None, :]
    scores = (
        jnp.einsum("hpbd,hpnd->hpbn", query_blk, key_list, preferred_element_type=jnp.float32)
        * score_scale
    )
    scores = jnp.where(key_mask, scores, NEGATIVE)
    row_top = jnp.max(scores, axis=3, keepdims=True)
    expo_vals = jnp.where(key_mask, jnp.exp(scores - row_top), 0.0)
    row_total = jnp.sum(expo_vals, axis=3, keepdims=True)
    numerator = jnp.einsum(
        "hpbn,hpnd->hpbd",
        expo_vals.astype(jnp.bfloat16),
        value_list,
        preferred_element_type=jnp.float32,
    )
    attended = (numerator / row_total).astype(jnp.bfloat16)
    row_delta = jnp.sum(grad_blk.astype(jnp.float32) * attended.astype(jnp.float32), axis=3)
    weights = expo_vals / row_total * keep_rows[None, :, None, None]
    dprobs = jnp.einsum("hpbd,hpnd->hpbn", grad_blk, value_list, preferred_element_type=jnp.float32)
    dscores = (weights * (dprobs - row_delta[:, :, :, None]) * score_scale).astype(jnp.bfloat16)
    dquery = jnp.einsum("hpbn,hpnd->hpbd", dscores, key_list, preferred_element_type=jnp.float32)
    key_global, key_padded, key_random = spread_terms(dscores, query_blk)
    value_global, value_padded, value_random = spread_terms(weights.astype(jnp.bfloat16), grad_blk)
    global_part = jnp.stack([key_global, value_global], axis=1)
    padded = jnp.stack([key_padded, value_padded], axis=1)
    random_part = jnp.stack([key_random, value_random], axis=1)
    return (attended, dquery, global_part, padded, random_part)


def shards(queries, keys, values, key_gain, random_blocks, out_grad):
    score_scale = HD ** (-0.5)
    tok_count = queries.shape[1]
    per_dev = tok_count // BLOCK
    owners = lax.axis_size("seq")
    seq_place = lax.axis_index("seq")
    total_blocks = owners * per_dev
    first_block = seq_place * per_dev
    key_eff = (keys[0].astype(jnp.float32) * key_gain).astype(jnp.bfloat16)
    edge_count = NG * BLOCK
    edge_rows = broadcast(
        jnp.stack(
            [
                queries[0, :edge_count],
                key_eff[:edge_count],
                values[0, :edge_count],
                out_grad[0, :edge_count],
            ]
        ),
        "seq",
        0,
    )
    window_rows = padded_2(jnp.stack([key_eff, values[0]]), (("seq", 1),), BLOCK)
    query_h = to_heads(queries[0])
    key_h = to_heads(key_eff)
    value_h = to_heads(values[0])
    grad_h = to_heads(out_grad[0])
    edge_heads = [to_heads(edge_rows[slot_pick]) for slot_pick in range(4)]
    window_key = to_heads(window_rows[0])
    window_value = to_heads(window_rows[1])
    request_count = HEADS * per_dev * NR
    capacity = (request_count + owners - 1) // owners + 3
    target = random_blocks.reshape(request_count)
    owner_dev = target // per_dev
    table_index = (
        jnp.arange(request_count, dtype=jnp.int32) // (per_dev * NR) * per_dev + target % per_dev
    )
    onehot = (owner_dev[:, None] == jnp.arange(owners, dtype=jnp.int32)[None, :]).astype(jnp.int32)
    before = jnp.cumsum(onehot, axis=0) - onehot
    slot_rank = jnp.sum(before * onehot, axis=1)
    position = owner_dev * capacity + slot_rank
    outgoing = (
        jnp.full((owners * capacity,), -1, jnp.int32)
        .at[position]
        .set(table_index)
        .reshape(owners, capacity)
    )
    kv_table = jnp.concatenate([key_h, value_h], axis=3).reshape(HEADS * per_dev, BLOCK, 2 * HD)
    index_part = lax.all_to_all(outgoing, "seq", split_axis=0, concat_axis=0, tiled=True)
    picked = kv_table[jnp.clip(index_part, 0, HEADS * per_dev - 1)]
    fetch_result = (
        lax.all_to_all(picked, "seq", split_axis=0, concat_axis=0, tiled=True),
        index_part,
    )
    arrived, served = fetch_result
    fetched = arrived.reshape(owners * capacity, BLOCK, 2 * HD)[position].reshape(
        HEADS, per_dev, NR, BLOCK, 2 * HD
    )
    fetched_key = fetched[..., :HD]
    fetched_value = fetched[..., HD:]
    block_index = first_block + jnp.arange(per_dev, dtype=jnp.int32)
    window_index = block_index[:, None] + jnp.arange(-1, 2, dtype=jnp.int32)[None, :]
    valid_keys = jnp.concatenate(
        [
            jnp.ones((per_dev, NG), bool),
            (window_index >= NG) & (window_index < total_blocks),
            jnp.ones((per_dev, NR), bool),
        ],
        axis=1,
    )
    keep_rows = (block_index >= NG).astype(jnp.float32)
    group_size = math.gcd(HEADS, 4)

    def by_group(array_in):
        return array_in.reshape((HEADS // group_size, group_size) + array_in.shape[1:])

    def merge_groups(array_in):
        return array_in.reshape((HEADS,) + array_in.shape[2:])

    def run_group(bundle):
        return sparse_group(
            bundle[0],
            bundle[1],
            bundle[2],
            bundle[3],
            bundle[4],
            bundle[5],
            bundle[6],
            bundle[7],
            valid_keys,
            keep_rows,
        )

    grouped = lax.map(
        run_group,
        (
            by_group(query_h),
            by_group(edge_heads[1]),
            by_group(edge_heads[2]),
            by_group(window_key),
            by_group(window_value),
            by_group(fetched_key),
            by_group(fetched_value),
            by_group(grad_h),
        ),
    )
    attended_h, dquery_h, global_part, padded, random_part = [
        merge_groups(piece_out) for piece_out in grouped
    ]
    edge_query = edge_heads[0].reshape(HEADS, edge_count, HD)
    edge_grad = edge_heads[3].reshape(HEADS, edge_count, HD)
    flat_key = key_h.reshape(HEADS, tok_count, HD)
    flat_value = value_h.reshape(HEADS, tok_count, HD)
    edge_scores = (
        jnp.einsum("hqd,htd->hqt", edge_query, flat_key, preferred_element_type=jnp.float32)
        * score_scale
    )
    edge_top = lax.pmax(jnp.max(edge_scores, axis=2), "seq")
    edge_expo = jnp.exp(edge_scores - edge_top[:, :, None])
    edge_total, edge_numer = lax.psum(
        (
            jnp.sum(edge_expo, axis=2),
            jnp.einsum(
                "hqt,htd->hqd",
                edge_expo.astype(jnp.bfloat16),
                flat_value,
                preferred_element_type=jnp.float32,
            ),
        ),
        "seq",
    )
    edge_out = (edge_numer / edge_total[:, :, None]).astype(jnp.bfloat16)
    edge_delta = jnp.sum(edge_grad.astype(jnp.float32) * edge_out.astype(jnp.float32), axis=2)
    edge_weights = edge_expo / edge_total[:, :, None]
    edge_dprobs = jnp.einsum(
        "hqd,htd->hqt", edge_grad, flat_value, preferred_element_type=jnp.float32
    )
    edge_dscores = (edge_weights * (edge_dprobs - edge_delta[:, :, None]) * score_scale).astype(
        jnp.bfloat16
    )
    edge_dquery = jnp.einsum(
        "hqt,htd->hqd", edge_dscores, flat_key, preferred_element_type=jnp.float32
    )
    local_dkey = jnp.einsum(
        "hqt,hqd->htd", edge_dscores, edge_query, preferred_element_type=jnp.float32
    )
    local_dvalue = jnp.einsum(
        "hqt,hqd->htd",
        edge_weights.astype(jnp.bfloat16),
        edge_grad,
        preferred_element_type=jnp.float32,
    )
    random_rounded = (
        random_part.transpose(0, 2, 3, 4, 1, 5)
        .reshape(request_count, BLOCK, 2 * HD)
        .astype(jnp.bfloat16)
    )
    sendback = (
        jnp.zeros((owners * capacity, BLOCK, 2 * HD), jnp.bfloat16)
        .at[position]
        .set(random_rounded)
        .reshape(owners, capacity, BLOCK, 2 * HD)
    )
    returned = lax.all_to_all(sendback, "seq", split_axis=0, concat_axis=0, tiled=True)
    owner_table = (
        served.reshape(1, owners * capacity)
        == jnp.arange(HEADS * per_dev, dtype=jnp.int32)[:, None]
    ).astype(jnp.bfloat16)
    summed = jnp.dot(
        owner_table,
        returned.reshape(owners * capacity, BLOCK * 2 * HD),
        preferred_element_type=jnp.float32,
    )
    summed = summed.reshape(HEADS, per_dev, BLOCK, 2, HD).transpose(0, 3, 1, 2, 4)
    from_right = passed_along(padded[:, :, 0].astype(jnp.bfloat16), "seq", -1).astype(jnp.float32)
    from_left = passed_along(padded[:, :, per_dev + 1].astype(jnp.bfloat16), "seq", 1).astype(
        jnp.float32
    )
    edge_dquery_sum, global_sum = lax.psum((edge_dquery, global_part), "seq")
    accum = padded[:, :, 1 : per_dev + 1]
    accum = accum + jnp.stack([local_dkey, local_dvalue], axis=1).reshape(
        HEADS, 2, per_dev, BLOCK, HD
    )
    accum = accum + summed
    accum = accum.at[:, :, per_dev - 1].add(from_right)
    accum = accum.at[:, :, 0].add(from_left)
    is_first = (seq_place == 0).astype(jnp.float32)
    accum = accum.at[:, :, :NG].add(global_sum * is_first)
    is_edge = (block_index < NG)[None, :, None, None]
    tail_zeros = jnp.zeros((HEADS, per_dev - NG, BLOCK, HD), jnp.float32)
    edge_dq_blocks = jnp.concatenate(
        [edge_dquery_sum.reshape(HEADS, NG, BLOCK, HD), tail_zeros], axis=1
    )
    edge_out_blocks = jnp.concatenate(
        [edge_out.reshape(HEADS, NG, BLOCK, HD), tail_zeros.astype(jnp.bfloat16)], axis=1
    )
    dquery_all = jnp.where(is_edge, edge_dq_blocks, dquery_h).astype(jnp.bfloat16)
    attended_all = jnp.where(is_edge, edge_out_blocks, attended_h)
    key_eff_grad = accum[:, 0]
    gain_heads = key_gain.reshape(HEADS, HD)
    key_grad_h = (key_eff_grad * gain_heads[:, None, None, :]).astype(jnp.bfloat16)
    value_grad_h = accum[:, 1].astype(jnp.bfloat16)
    gain_term = jnp.sum(key_eff_grad * to_heads(keys[0]).astype(jnp.float32), axis=(1, 2)).reshape(
        HEADS * HD
    )
    gain_grad = lax.psum(gain_term, ("dp", "seq"))
    return (
        from_heads(attended_all),
        from_heads(dquery_all),
        from_heads(key_grad_h),
        from_heads(value_grad_h),
        gain_grad,
    )


def solution(mesh):
    placed = (
        P("dp", "seq", None),
        P("dp", "seq", None),
        P("dp", "seq", None),
        P(),
        P(None, "seq", None),
        P("dp", "seq", None),
    )
    return jax.shard_map(
        shards,
        mesh=mesh,
        in_specs=placed,
        out_specs=(
            P("dp", "seq", None),
            P("dp", "seq", None),
            P("dp", "seq", None),
            P("dp", "seq", None),
            P(),
        ),
        check_vma=False,
    )
```

profile of v0, /device:TPU:1, one launch (start us, length us, event | category | flops | bytes accessed | tf_op | source)
XLA Modules:
  0.0 1441.6 jit_solution(389370633972243564)
XLA Ops:
  11.2 12.0 all-to-all-start
  33.7 10.3 gather_fusion
  43.9 7.5 all-to-all-start.1
  68.2 25.1 %collective-permute-done = bf16[2,64,2048]{2,1,0:T(8,128)(2,1)} collective-permute-done((bf16[2,64,2048]{2,1,0:T(8,128)(2,1)}, bf16[2,64,2048]{2,1,0:T(8,128)(2,1)}, u32[]{:S(2)}, u32[]{:S(2)}) %collective-permute-start) | collective-permute-done | bytes 524320 | tf_op jit(solution)/shard_map/ppermute | solution.py:29
  93.3 21.3 %collective-permute-done.1 = bf16[2,64,2048]{2,1,0:T(8,128)(2,1)} collective-permute-done((bf16[2,64,2048]{2,1,0:T(8,128)(2,1)}, bf16[2,64,2048]{2,1,0:T(8,128)(2,1)}, u32[]{:S(2)}, u32[]{:S(2)}) %collective-permute-start.1) | collective-permute-done | bytes 524320 | tf_op jit(solution)/shard_map/ppermute | solution.py:31
  119.1 206.0 %all-reduce.14.cloned.1.call-done = bf16[4,128,2048]{2,1,0:T(8,128)(2,1)} async-done(((bf16[4,128,2048]{2,1,0:T(8,128)(2,1)}), bf16[4,128,2048]{2,1,0:T(8,128)(2,1)}) %all-reduce.14.cloned.1.call-update) | async-done | bytes 2097168 | tf_op jit(solution)/shard_map/psum | solution.py:18
  329.1 11.8 gather_fusion.1
  340.9 8.0 fusion.134
  348.9 287.8 %while.24 = (s32[]{:T(128)}, bf16[4,4,4,64,128]{4,3,2,1,0:T(8,128)(2,1)}, bf16[4,4,4,64,128]{4,3,2,1,0:T(8,128)(2,1)}, f32[4,4,2,2,64,128]{5,1,0,2,4,3:T(4,128)}...) while((s32[]{:T(128)}, ...), condition=%wide.region_14.15_spmd.clone, body=%wide.region_10.14_spmd.clone.sunk | while | flops 952370176 | bytes 142396560 | solution.py:227
  368.6 5.1 bitcast_dynamic-update-slice_fusion.6
  440.4 5.1 bitcast_dynamic-update-slice_fusion.6
  584.1 5.1 bitcast_dynamic-update-slice_fusion.6
  636.7 12.7 copy.168
  649.4 10.8 reshape.529
  665.1 29.1 %scatter_fusion = bf16[288,64,256]{2,1,0:T(8,128)(2,1)} fusion(bf16[288,64,256]{2,1,0:T(8,128)(2,1)} %broadcast_in_dim.167, s32[192]{0:T(256)S(1)} %bitcast.511, bf16[192,64,256]{2,1,0:T(8,128)(2,1)} %reshape.529), kind=kCustom, calls=%fused_computation.3 | custom fusion | bytes 18875136 | tf_op jit(solution)/shard_map/scatter | solution.py:294
  694.3 6.0 all-to-all-start.2
  704.3 248.7 %pmax.7 = f32[16,128]{1,0:T(8,128)S(1)} all-reduce(f32[16,128]{1,0:T(8,128)S(1)} %get-tuple-element.352), channel_id=1, replica_groups=mesh['dp'=8,'seq'=32] {'seq'}, use_global_device_ids=true, to_apply=%region_2.3 | all-reduce | flops 2048 | bytes 16384 | tf_op jit(solution)/shard_map/pmax | solution.py:251
  960.4 59.2 %psum.44 = f32[16,128]{1,0:T(8,128)S(1)} all-reduce(f32[16,128]{1,0:T(8,128)S(1)} %fusion.95), channel_id=1, replica_groups=mesh['dp'=8,'seq'=32] {'seq'}, use_global_device_ids=true, to_apply=%region_5.6 | all-reduce | flops 2048 | bytes 16384 | tf_op jit(solution)/shard_map/psum | solution.py:253
  1033.0 99.2 %all-reduce.16.cloned.1.call-done = (f32[16,128,128]{2,1,0:T(8,128)}, f32[16,2,2,64,128]{4,0,1,3,2:T(8,128)}) async-done(((f32[16,128,128]{2,1,0:T(8,128)}, f32[16,2,2,64,128]{4,0,1,3,2:T(8,128)}), (f32[16,128,128]{2,1,0:T(8,128)}, f32[16,2,2,64,128]{4,0,1,3,2:T(8,128)})) %all-reduce.16.cloned.1.call-update) | async-done | bytes 3145744 | tf_op jit(solution)/shard_map/psum | solution.py:253
  1141.9 123.4 %all-reduce.17 = bf16[16,2,64,128]{3,2,1,0:T(8,128)(2,1)S(1)} all-reduce(f32[16,2,64,128]{3,2,1,0:T(8,128)} %bitcast.485), channel_id=1, replica_groups=mesh['dp'=8,'seq'=32] {'seq'}, use_global_device_ids=true, to_apply=%region_16.17 | all-reduce | flops 262144 | bytes 1572864 | tf_op jit(solution)/shard_map/psum | solution.py:312
  1273.5 18.5 %copy.212 = bf16[36,8,64,256]{3,1,2,0:T(8,128)(2,1)} copy(bf16[36,8,64,256]{3,2,1,0:T(8,128)(2,1)} %bitcast.182) | data formatting | bytes 18874368
  1292.0 16.1 %dot_general.116 = bf16[64,2,128,288]{2,1,0,3:T(2,128)(2,1)} reshape(bf16[16384,288]{0,1:T(8,128)(2,1)} %bitcast.460) | data formatting | bytes 18874368 | tf_op jit(solution)/shard_map/dot_general | solution.py:302
  1308.1 12.3 fusion.85
  1328.3 106.2 %psum.47 = f32[2048]{0:T(1024)} all-reduce(f32[2048]{0:T(1024)S(1)} %bitcast.508), channel_id=1, replica_groups=mesh['dp'=8,'seq'=32] {'dp','seq'}, use_global_device_ids=true, to_apply=%region_20.21 | all-reduce | flops 2048 | bytes 16384 | tf_op jit(solution)/shard_map/psum | solution.py:339
  (477 shorter events, 365.1 us)
Async XLA Ops:
  9.3 58.8 %copy-start.31 = (s32[192,1]{0,1:T(1,128)}, s32[192,1]{0,1:T(1,128)S(1)}, u32[]{:S(2)}) copy-start(s32[192,1]{0,1:T(1,128)S(1)} %compare_select_fusion.1) | copy-start | bytes 2308
  11.2 20.6 %all-to-all-start = ((s32[32,1,9]{2,1,0:T(1,128)}), s32[32,1,9]{2,1,0:T(1,128)S(1)}, u32[]{:S(2)}, u32[]{:S(2)}) async-start(s32[32,1,9]{2,1,0:T(1,128)} %bitcast.20), calls=%async_computation | async-start | bytes 32768 | tf_op jit(solution)/shard_map/all_to_all | solution.py:182
  43.9 285.2 %all-to-all-start.1 = ((bf16[32,9,64,256]{3,2,1,0:T(8,128)(2,1)}), bf16[32,9,64,256]{3,2,1,0:T(8,128)(2,1)}, u32[]{:S(2)}, u32[]{:S(2)}) async-start(bf16[32,9,64,256]{3,2,1,0:T(8,128)(2,1)} %bitcast.459), calls=%async_computation.1 | async-start | bytes 18874368 | tf_op jit(solution)/shard_map/all_to_all | solution.py:185
  51.4 273.7 %all-reduce.14.cloned.1.call-start = ((), (), s32[]{:S(2)}) async-start(), calls=%async_computation.3 | async-start | bytes 4194304 | tf_op jit(solution)/shard_map/psum | solution.py:18
  58.0 35.3 %collective-permute-start = (bf16[2,64,2048]{2,1,0:T(8,128)(2,1)}, bf16[2,64,2048]{2,1,0:T(8,128)(2,1)}, u32[]{:S(2)}, u32[]{:S(2)}) collective-permute-start(bf16[2,64,2048]{2,1,0:T(8,128)(2,1)} %get-tuple-element.342), channel_id=1, source_target_pairs={{0,1},{1,2},{2,3},{3,4},{4,5},{5,6},{6,7},{7,8},{8,9},{9,10},{10,1... | collective-permute-start | bytes 1572872 | tf_op jit(solution)/shard_map/ppermute | solution.py:29
  61.8 52.8 %collective-permute-start.1 = (bf16[2,64,2048]{2,1,0:T(8,128)(2,1)}, bf16[2,64,2048]{2,1,0:T(8,128)(2,1)}, u32[]{:S(2)}, u32[]{:S(2)}) collective-permute-start(bf16[2,64,2048]{2,1,0:T(8,128)(2,1)} %get-tuple-element.343), channel_id=1, source_target_pairs={{1,0},{2,1},{3,2},{4,3},{5,4},{6,5},{7,6},{8,7},{9,8},{10,9},{11,1... | collective-permute-start | bytes 1572872 | tf_op jit(solution)/shard_map/ppermute | solution.py:31
  355.9 3.7 copy-start.1
  380.2 3.8 copy-start.5
  427.7 3.7 copy-start.1
  452.0 3.8 copy-start.5
  499.5 3.7 copy-start.1
  523.8 3.8 copy-start.5
  526.0 3.0 copy-start
  571.3 3.7 copy-start.1
  595.6 3.8 copy-start.5
  660.3 4.9 copy-start.32
  694.3 6.1 copy-start.7
  694.3 6.1 copy-start.29
  694.3 579.3 %all-to-all-start.2 = ((bf16[32,9,64,256]{3,2,1,0:T(8,128)(2,1)}), bf16[32,9,64,256]{3,2,1,0:T(8,128)(2,1)}, u32[]{:S(2)}, u32[]{:S(2)}) async-start(bf16[32,9,64,256]{3,2,1,0:T(8,128)(2,1)} %bitcast.457), calls=%async_computation.2 | async-start | bytes 18874368 | tf_op jit(solution)/shard_map/all_to_all | solution.py:297
  700.3 432.0 %all-reduce.16.cloned.1.call-start = ((), (), s32[]{:S(2)}) async-start(), calls=%async_computation.4 | async-start | bytes 6291456 | tf_op jit(solution)/shard_map/psum | solution.py:253
  1019.5 5.5 slice-start.1
  1019.5 5.5 slice-start.2
  1026.9 293.5 %collective-permute-start.2 = (bf16[16,2,64,128]{3,0,1,2:T(8,128)(2,1)}, bf16[16,2,64,128]{3,0,1,2:T(8,128)(2,1)}, u32[]{:S(2)}, u32[]{:S(2)}) collective-permute-start(bf16[16,2,64,128]{3,0,1,2:T(8,128)(2,1)} %get-tuple-element.335), channel_id=1, source_target_pairs={{1,0},{2,1},{3,2},{4,3},{5,4},{6,5},{7,6},{8,7},{9,8},{10,9},{11,1... | collective-permute-start | bytes 1572872 | tf_op jit(solution)/shard_map/ppermute | solution.py:41
  1028.2 293.7 %collective-permute-start.3 = (bf16[16,2,64,128]{3,0,1,2:T(8,128)(2,1)}, bf16[16,2,64,128]{3,0,1,2:T(8,128)(2,1)}, u32[]{:S(2)}, u32[]{:S(2)}) collective-permute-start(bf16[16,2,64,128]{3,0,1,2:T(8,128)(2,1)} %get-tuple-element.334), channel_id=1, source_target_pairs={{0,1},{1,2},{2,3},{3,4},{4,5},{5,6},{6,7},{7,8},{8,9},{9,10},{10,1... | collective-permute-start | bytes 1572872 | tf_op jit(solution)/shard_map/ppermute | solution.py:41
  (65 other events, 121.0 us)
Sparse Core Ops, SparseCore 0:
  55.8 269.2 all-reduce.13
  956.7 175.5 all-reduce.15
where the time goes:
time: 1450 us; the launch traced here: 1440 us
  blocking collectives  538 us (37%)
  waiting for transfers between devices  353 us (24%)
  local copies, waits for them, and re-layouts  289 us (20%)
  matrix products  154 us (11%)
  other arithmetic  53.4 us (4%)
  starting transfers between devices  37.3 us (3%)
  between operations  14.9 us (1%)
    pmax x1, blocking collectives, shards(): edge_top = lax.pmax(jnp.max(edge_scores, axis=2), 'seq')  249 us
    psum x1, waiting for transfers between devices, broadcast(): return lax.psum(block, axis)  206 us
    psum x1, blocking collectives, shards(): edge_dquery_sum, global_sum = lax.psum((edge_dquery, global_part), 'seq')  123 us
    psum x1, blocking collectives, shards(): gain_grad = lax.psum(gain_term, ('dp', 'seq'))  106 us
    psum x1, waiting for transfers between devices, shards(): lax.psum((jnp.sum(edge_expo, axis=2), jnp.einsum('hqt,htd->hqd', edge_exp...  99.2 us
    psum x1, blocking collectives, shards(): lax.psum((jnp.sum(edge_expo, axis=2), jnp.einsum('hqt,htd->hqd', edge_exp...  59.2 us
    while x160, local copies, waits for them, and re-layouts  46.8 us
    dot_general x24, matrix products, spread_terms(): jnp.einsum('hpbc,hpbd->hpcd', coef_blocks[:, :, :, NG + offset], rows_in,...  41.4 us
  transfers between devices with their start and end apart: 9, of which 5 were waited for; matrix products, arithmetic and copies ran while one was open for 7% of the time, Pallas kernels for 0%

commit v1 on v0

--- a/solution.py
+++ b/solution.py
@@ -15,7 +15,7 @@
 
 def broadcast(block, axis, owner):
     block = jnp.where(lax.axis_index(axis) == owner, block, jnp.zeros_like(block))
-    return lax.psum(block, axis)
+    return jnp.sum(lax.all_gather(block, axis), axis=0)
 
 
 def padded_2(cells, sides, width):

time: 1450 us -> 1770 us (1.22)
  waiting for transfers between devices: 353 us -> 649 us
  other arithmetic: 53.4 us -> 76.3 us
    all_gather x0 -> x1, waiting for transfers between devices: none -> 292 us  [broadcast(): return jnp.sum(lax.all_gather(block, axis), axis=0)]
    all_to_all x1, waiting for transfers between devices: 0.01 us -> 217 us  [shards(): lax.all_to_all(picked, 'seq', split_axis=0, concat_axis=0, tiled=True)]
    psum x1 -> x0, waiting for transfers between devices: 206 us -> none  [broadcast(): return lax.psum(block, axis)]
    reduce_sum x0 -> x1, other arithmetic: none -> 21.3 us  [broadcast(): return jnp.sum(lax.all_gather(block, axis), axis=0)]
    while x160 -> x144, local copies, waits for them, and re-layouts: 46.8 us -> 40.9 us
  transfers between devices with their start and end apart: 9 -> 9, of which waited for: 5 -> 6; matrix products, arithmetic and copies ran while one was open for 7% -> 7% of each run, Pallas kernels for 0% -> 0%
where the time goes in v1:
time: 1770 us; the launch traced here: 1760 us
  waiting for transfers between devices  649 us (37%)
  blocking collectives  546 us (31%)
  local copies, waits for them, and re-layouts  286 us (16%)
  matrix products  154 us (9%)
  other arithmetic  76.3 us (4%)
  starting transfers between devices  34.7 us (2%)
    all_gather x1, waiting for transfers between devices, broadcast(): return jnp.sum(lax.all_gather(block, axis), axis=0)  292 us
    pmax x1, blocking collectives, shards(): edge_top = lax.pmax(jnp.max(edge_scores, axis=2), 'seq')  259 us
    all_to_all x1, waiting for transfers between devices, shards(): lax.all_to_all(picked, 'seq', split_axis=0, concat_axis=0, tiled=True)  217 us
    psum x1, blocking collectives, shards(): edge_dquery_sum, global_sum = lax.psum((edge_dquery, global_part), 'seq')  123 us
    psum x1, blocking collectives, shards(): gain_grad = lax.psum(gain_term, ('dp', 'seq'))  106 us
    psum x1, waiting for transfers between devices, shards(): lax.psum((jnp.sum(edge_expo, axis=2), jnp.einsum('hqt,htd->hqd', edge_exp...  90.8 us
    psum x1, blocking collectives, shards(): lax.psum((jnp.sum(edge_expo, axis=2), jnp.einsum('hqt,htd->hqd', edge_exp...  57.5 us
    dot_general x24, matrix products, spread_terms(): jnp.einsum('hpbc,hpbd->hpcd', coef_blocks[:, :, :, NG + offset], rows_in,...  41 us
  transfers between devices with their start and end apart: 9, of which 6 were waited for; matrix products, arithmetic and copies ran while one was open for 7% of the time, Pallas kernels for 0%

profile of v1, /device:TPU:1, one launch (start us, length us, event | category | flops | bytes accessed | tf_op | source)
XLA Modules:
  0.0 1762.9 jit_solution(6948329964176191230)
XLA Ops:
  19.5 12.0 all-to-all-start
  34.8 5.3 all-to-all-done
  42.0 10.3 gather_fusion
  52.3 5.1 all-to-all-start.1
  68.8 36.9 %collective-permute-done = bf16[2,64,2048]{2,1,0:T(8,128)(2,1)} collective-permute-done((bf16[2,64,2048]{2,1,0:T(8,128)(2,1)}, bf16[2,64,2048]{2,1,0:T(8,128)(2,1)}, u32[]{:S(2)}, u32[]{:S(2)}) %collective-permute-start) | collective-permute-done | bytes 524320 | tf_op jit(solution)/shard_map/ppermute | solution.py:29
  105.7 7.5 collective-permute-done.1
  119.4 217.3 %all-to-all-done.1 = bf16[32,9,64,256]{3,2,1,0:T(8,128)(2,1)} async-done(((bf16[32,9,64,256]{3,2,1,0:T(8,128)(2,1)}), bf16[32,9,64,256]{3,2,1,0:T(8,128)(2,1)}, u32[]{:S(2)}, u32[]{:S(2)}) %all-to-all-start.1) | async-done | bytes 9437216 | tf_op jit(solution)/shard_map/all_to_all | solution.py:185
  336.8 11.8 gather_fusion.1
  348.6 8.3 fusion.134
  356.9 291.6 %all-gather.2.cloned.1.call-done = bf16[32,4,128,2048]{3,2,1,0:T(8,128)(2,1)} async-done(((bf16[1,4,128,2048]{3,2,1,0:T(8,128)(2,1)}), bf16[32,4,128,2048]{3,2,1,0:T(8,128)(2,1)}) %all-gather.2.cloned.1.call-update) | async-done | bytes 67108880 | tf_op jit(solution)/shard_map/all_gather | solution.py:18
  648.5 21.3 %reduce_sum.74 = bf16[4,128,2048]{2,1,0:T(8,128)(2,1)S(1)} reduce(bf16[32,4,128,2048]{3,2,1,0:T(8,128)(2,1)} %all-gather.2.cloned.1.call-done, bf16[]{:T(256)} %constant.203.clone.1), dimensions={0}, to_apply=%region_0.1 | reduce | flops 32505856 | bytes 69206016 | tf_op jit(solution)/shard_map/reduce_sum | solution.py:18
  672.0 286.4 %while.24 = (s32[]{:T(128)}, bf16[4,4,4,64,128]{4,3,2,1,0:T(8,128)(2,1)}, bf16[4,4,4,64,128]{4,3,2,1,0:T(8,128)(2,1)}, f32[4,4,2,2,64,128]{5,1,0,2,4,3:T(4,128)}...) while((s32[]{:T(128)}, ...), condition=%wide.region_14.15_spmd.clone, body=%wide.region_10.14_spmd.clone.sunk | while | flops 952370176 | bytes 130337880 | solution.py:227
  958.4 12.7 copy.164
  971.1 10.8 reshape.585
  986.7 28.9 %scatter_fusion = bf16[288,64,256]{2,1,0:T(8,128)(2,1)} fusion(bf16[288,64,256]{2,1,0:T(8,128)(2,1)} %broadcast_in_dim.167, s32[192]{0:T(256)S(1)} %bitcast.529, bf16[192,64,256]{2,1,0:T(8,128)(2,1)} %reshape.585), kind=kCustom, calls=%fused_computation.3 | custom fusion | bytes 18875136 | tf_op jit(solution)/shard_map/scatter | solution.py:294
  1015.6 5.7 all-to-all-start.2
  1025.4 258.8 %pmax.7 = f32[16,128]{1,0:T(8,128)S(1)} all-reduce(f32[16,128]{1,0:T(8,128)S(1)} %get-tuple-element.400), channel_id=1, replica_groups=mesh['dp'=8,'seq'=32] {'seq'}, use_global_device_ids=true, to_apply=%region_2.3 | all-reduce | flops 2048 | bytes 16384 | tf_op jit(solution)/shard_map/pmax | solution.py:251
  1291.6 57.5 %psum.36 = f32[16,128]{1,0:T(8,128)S(1)} all-reduce(f32[16,128]{1,0:T(8,128)S(1)} %fusion.95), channel_id=1, replica_groups=mesh['dp'=8,'seq'=32] {'seq'}, use_global_device_ids=true, to_apply=%region_5.6 | all-reduce | flops 2048 | bytes 16384 | tf_op jit(solution)/shard_map/psum | solution.py:253
  1362.8 90.8 %all-reduce.13.cloned.1.call-done = (f32[16,128,128]{2,1,0:T(8,128)}, f32[16,2,2,64,128]{4,0,1,3,2:T(8,128)}) async-done(((f32[16,128,128]{2,1,0:T(8,128)}, f32[16,2,2,64,128]{4,0,1,3,2:T(8,128)}), (f32[16,128,128]{2,1,0:T(8,128)}, f32[16,2,2,64,128]{4,0,1,3,2:T(8,128)})) %all-reduce.13.cloned.1.call-update) | async-done | bytes 3145744 | tf_op jit(solution)/shard_map/psum | solution.py:253
  1463.3 123.4 %all-reduce.14 = bf16[16,2,64,128]{3,2,1,0:T(8,128)(2,1)S(1)} all-reduce(f32[16,2,64,128]{3,2,1,0:T(8,128)} %bitcast.505), channel_id=1, replica_groups=mesh['dp'=8,'seq'=32] {'seq'}, use_global_device_ids=true, to_apply=%region_16.17 | all-reduce | flops 262144 | bytes 1572864 | tf_op jit(solution)/shard_map/psum | solution.py:312
  1594.9 18.5 %copy.210 = bf16[36,8,64,256]{3,1,2,0:T(8,128)(2,1)} copy(bf16[36,8,64,256]{3,2,1,0:T(8,128)(2,1)} %bitcast.181) | data formatting | bytes 18874368
  1613.4 16.1 dot_general.116
  1629.5 12.3 fusion.85
  1649.7 106.1 %psum.39 = f32[2048]{0:T(1024)} all-reduce(f32[2048]{0:T(1024)S(1)} %bitcast.526), channel_id=1, replica_groups=mesh['dp'=8,'seq'=32] {'dp','seq'}, use_global_device_ids=true, to_apply=%region_20.21 | all-reduce | flops 2048 | bytes 16384 | tf_op jit(solution)/shard_map/psum | solution.py:339
  (469 shorter events, 376.9 us)
Async XLA Ops:
  7.2 641.4 %all-gather.2.cloned.1.call-start = ((), (), s32[]{:S(2)}) async-start(), calls=%async_computation.3 | async-start | bytes 69206016 | tf_op jit(solution)/shard_map/all_gather | solution.py:18
  7.2 4.0 copy-start.25
  17.6 51.1 %copy-start.28 = (s32[192,1]{0,1:T(1,128)}, s32[192,1]{0,1:T(1,128)S(1)}, u32[]{:S(2)}) copy-start(s32[192,1]{0,1:T(1,128)S(1)} %compare_select_fusion.1) | copy-start | bytes 2308
  19.5 20.6 %all-to-all-start = ((s32[32,1,9]{2,1,0:T(1,128)}), s32[32,1,9]{2,1,0:T(1,128)S(1)}, u32[]{:S(2)}, u32[]{:S(2)}) async-start(s32[32,1,9]{2,1,0:T(1,128)} %bitcast.23), calls=%async_computation | async-start | bytes 32768 | tf_op jit(solution)/shard_map/all_to_all | solution.py:182
  52.3 5.1 copy-start.14
  52.3 284.5 %all-to-all-start.1 = ((bf16[32,9,64,256]{3,2,1,0:T(8,128)(2,1)}), bf16[32,9,64,256]{3,2,1,0:T(8,128)(2,1)}, u32[]{:S(2)}, u32[]{:S(2)}) async-start(bf16[32,9,64,256]{3,2,1,0:T(8,128)(2,1)} %bitcast.477), calls=%async_computation.1 | async-start | bytes 18874368 | tf_op jit(solution)/shard_map/all_to_all | solution.py:185
  58.7 47.0 %collective-permute-start = (bf16[2,64,2048]{2,1,0:T(8,128)(2,1)}, bf16[2,64,2048]{2,1,0:T(8,128)(2,1)}, u32[]{:S(2)}, u32[]{:S(2)}) collective-permute-start(bf16[2,64,2048]{2,1,0:T(8,128)(2,1)} %get-tuple-element.390), channel_id=1, source_target_pairs={{0,1},{1,2},{2,3},{3,4},{4,5},{5,6},{6,7},{7,8},{8,9},{9,10},{10,1... | collective-permute-start | bytes 1572872 | tf_op jit(solution)/shard_map/ppermute | solution.py:29
  62.5 50.7 %collective-permute-start.1 = (bf16[2,64,2048]{2,1,0:T(8,128)(2,1)}, bf16[2,64,2048]{2,1,0:T(8,128)(2,1)}, u32[]{:S(2)}, u32[]{:S(2)}) collective-permute-start(bf16[2,64,2048]{2,1,0:T(8,128)(2,1)} %get-tuple-element.391), channel_id=1, source_target_pairs={{1,0},{2,1},{3,2},{4,3},{5,4},{6,5},{7,6},{8,7},{9,8},{10,9},{11,1... | collective-permute-start | bytes 1572872 | tf_op jit(solution)/shard_map/ppermute | solution.py:31
  679.0 3.6 copy-start.1
  703.2 3.8 copy-start.5
  750.5 3.6 copy-start.1
  774.7 3.8 copy-start.5
  821.8 3.6 copy-start.1
  846.0 3.8 copy-start.5
  917.6 3.8 copy-start.5
  981.9 4.8 copy-start.29
  1015.6 5.8 copy-start.7
  1015.6 5.8 copy-start.26
  1015.6 579.3 %all-to-all-start.2 = ((bf16[32,9,64,256]{3,2,1,0:T(8,128)(2,1)}), bf16[32,9,64,256]{3,2,1,0:T(8,128)(2,1)}, u32[]{:S(2)}, u32[]{:S(2)}) async-start(bf16[32,9,64,256]{3,2,1,0:T(8,128)(2,1)} %bitcast.475), calls=%async_computation.2 | async-start | bytes 18874368 | tf_op jit(solution)/shard_map/all_to_all | solution.py:297
  1021.3 432.3 %all-reduce.13.cloned.1.call-start = ((), (), s32[]{:S(2)}) async-start(), calls=%async_computation.4 | async-start | bytes 6291456 | tf_op jit(solution)/shard_map/psum | solution.py:253
  1349.1 5.5 slice-start.1
  1349.1 5.5 slice-start.2
  1356.5 285.3 %collective-permute-start.2 = (bf16[16,2,64,128]{3,0,1,2:T(8,128)(2,1)}, bf16[16,2,64,128]{3,0,1,2:T(8,128)(2,1)}, u32[]{:S(2)}, u32[]{:S(2)}) collective-permute-start(bf16[16,2,64,128]{3,0,1,2:T(8,128)(2,1)} %get-tuple-element.383), channel_id=1, source_target_pairs={{1,0},{2,1},{3,2},{4,3},{5,4},{6,5},{7,6},{8,7},{9,8},{10,9},{11,1... | collective-permute-start | bytes 1572872 | tf_op jit(solution)/shard_map/ppermute | solution.py:41
  1357.8 285.5 %collective-permute-start.3 = (bf16[16,2,64,128]{3,0,1,2:T(8,128)(2,1)}, bf16[16,2,64,128]{3,0,1,2:T(8,128)(2,1)}, u32[]{:S(2)}, u32[]{:S(2)}) collective-permute-start(bf16[16,2,64,128]{3,0,1,2:T(8,128)(2,1)} %get-tuple-element.382), channel_id=1, source_target_pairs={{0,1},{1,2},{2,3},{3,4},{4,5},{5,6},{6,7},{7,8},{8,9},{9,10},{10,1... | collective-permute-start | bytes 1572872 | tf_op jit(solution)/shard_map/ppermute | solution.py:41
  (55 other events, 112.3 us)
Sparse Core Ops, SparseCore 0:
  15.6 632.8 all-gather.1
  1287.9 165.6 all-reduce.12
